TPU v7x, 256 devices: a whole 4x4x8 slice. The times are simulated.
256 devices in a mesh: row: 8 (over z), col: 8 (over y, core), tensor: 4 (over x).
Axes of the slice: x: 4, y: 4, z: 8, core: 2. Of those that a mesh axis runs over, the one named last changes fastest.
Arguments:
- hidden: bfloat16 [3072, 16, 11008], P(('row', 'col'), None, 'tensor'), may hold values from -6 to 6
- cotangent: bfloat16 [3072, 16, 4096], P(('row', 'col'), None, 'tensor'), may hold values from -6 to 6
- tile_live: int32 [64, 2], P(('row', 'col')), may hold values 0 or 1
Outputs:
- ntk_tiles: float32 [64, 2, 48, 48], P(('row', 'col'), None, 'tensor')
All inputs are finite; a program needn't handle non-finite values. No bound on the sum of `tile_live` on one device may be relied on, other than what follows from the above.
Results may differ from a plain program's by a relative error of at most 0.0003.
Values may be sent and summed in bfloat16 or wider, within the bound.
A program may use at most 64 MiB of HBM per device.

v0:
```python
import functools
import math

import jax
import jax.numpy as jnp
from jax import lax
from jax.sharding import PartitionSpec as P

D = 4096
FF = 11008


def from_behind(value, axis, steps):
    count = lax.axis_size(axis)
    pairs = [(source, (source + steps) % count) for source in range(count)]
    return lax.ppermute(value, axis, pairs)


def per_device(hidden, cotangent, tile_live):
    samples, tokens, hidden_width = hidden.shape
    cotan_width = cotangent.shape[2]
    block_rows = samples * tokens
    own_rows = (
        hidden.reshape(block_rows, hidden_width),
        cotangent.reshape(block_rows, cotan_width),
    )
    tensor_parts = lax.axis_size("tensor")
    share_rows = block_rows // tensor_parts
    kernel_scale = 1.0 / (tokens * math.sqrt(FF * D))
    live_flags = tile_live[0]
    tile_total = tile_live.shape[1]
    received = []
    current = own_rows
    for offset_step in range(tile_total):
        current = from_behind((current[0], current[1]), ("row", "col"), 1)
        received.append(current)

    def gram_terms(peer_rows, live_flag, row_start, row_count):
        rows_hidden = peer_rows[0]
        rows_cotan = peer_rows[1]

        def compute_tile(unused):
            gram_hidden = lax.dot_general(
                rows_hidden,
                own_rows[0],
                (((1,), (1,)), ((), ())),
                preferred_element_type=jnp.float32,
            )
            gram_cotan = lax.dot_general(
                rows_cotan,
                own_rows[1],
                (((1,), (1,)), ((), ())),
                preferred_element_type=jnp.float32,
            )
            return jnp.concatenate([gram_hidden, gram_cotan], axis=1)

        def skip_tile(unused):
            return jnp.zeros((row_count, 2 * block_rows), jnp.float32)

        return lax.cond(live_flag > 0, compute_tile, skip_tile, None)

    kernel_tiles = []
    for tile_index in range(tile_total):
        term_fn = functools.partial(gram_terms, received[tile_index], live_flags[tile_index])
        summed = lax.psum_scatter(
            term_fn(jnp.int32(0), lax.axis_size("tensor") * share_rows),
            "tensor",
            scatter_dimension=0,
            tiled=True,
        )
        left_gram = summed[:, :block_rows]
        right_gram = summed[:, block_rows:]
        product = (left_gram * right_gram).reshape(
            summed.shape[0] // tokens, tokens, samples, tokens
        )
        kernel_tiles.append(jnp.sum(product, axis=(1, 3)) * kernel_scale)
    return jnp.stack(kernel_tiles)[None]


def solution(mesh):
    placed = (
        P(("row", "col"), None, "tensor"),
        P(("row", "col"), None, "tensor"),
        P(("row", "col"), None),
    )
    return jax.shard_map(
        per_device,
        mesh=mesh,
        in_specs=placed,
        out_specs=P(("row", "col"), None, "tensor", None),
        check_vma=False,
    )
```

profile of v0, /device:TPU:2, one launch (start us, length us, event | category | flops | bytes accessed | tf_op | source)
XLA Modules:
  0.0 254.5 jit_solution(5440020056729821622)
XLA Ops:
  6.5 0.0 reduce-scatter.7.cloned.1.call-start
  6.5 0.0 copy-start.4
  6.5 0.0 copy-start
  6.5 6.6 %copy.16 = bf16[768,2752]{0,1:T(8,128)(2,1)} copy(bf16[768,2752]{1,0:T(8,128)(2,1)} %bitcast.18) | data formatting | bytes 8454144 | tf_op jit(solution)/shard_map/reshape | solution.py:24
  13.2 0.0 collective-permute-start
  13.2 0.0 copy-done.4
  13.2 1.7 collective-permute-start.1
  14.9 0.0 copy-done
  14.9 0.6 fusion.2
  16.1 68.4 %collective-permute-done.1 = bf16[768,1024]{1,0:T(8,128)(2,1)S(1)} collective-permute-done((bf16[768,1024]{1,0:T(8,128)(2,1)S(1)}, bf16[768,1024]{1,0:T(8,128)(2,1)S(1)}, u32[]{:S(2)}, u32[]{:S(2)}) %collective-permute-start.1) | collective-permute-done | bytes 1572896 | tf_op jit(solution)/shard_map/ppermute | solution.py:16
  84.5 0.0 collective-permute-done
  84.5 0.0 copy-start.1
  84.5 2.1 copy-done.1
  86.7 2.5 conditional.2
  86.7 2.5 broadcast.23
  89.1 6.1 %copy.24 = f32[768,1536]{1,0:T(8,128)} copy(f32[768,1536]{0,1:T(8,128)} %get-tuple-element.57) | data formatting | bytes 9437184
  95.2 0.0 reduce-scatter.7.cloned.1.call-update
  95.2 0.0 reduce-scatter.9.cloned.1.call-start
  95.3 0.1 collective-permute-start.2
  95.4 0.1 collective-permute-start.3
  96.0 71.7 %collective-permute-done.3 = bf16[768,1024]{1,0:T(8,128)(2,1)S(1)} collective-permute-done((bf16[768,1024]{1,0:T(8,128)(2,1)S(1)}, bf16[768,1024]{1,0:T(8,128)(2,1)S(1)}, u32[]{:S(2)}, u32[]{:S(2)}) %collective-permute-start.3) | collective-permute-done | bytes 1572896 | tf_op jit(solution)/shard_map/ppermute | solution.py:16
  167.8 0.0 collective-permute-done.2
  167.8 2.6 %conditional.3 = (f32[768,1536]{0,1:T(8,128)}) conditional(s32[]{:T(128)} %bitcast.4, () %tuple.19, (bf16[768,2752]{0,1:T(8,128)(2,1)S(1)}, bf16[768,2752]{1,0:T(8,128)(2,1)}, bf16[768,1024]{1,0:T(8,128)(2,1)S(1)}, bf16[768,1024]{1,0:T(8,128)(2,1)S(1)}) %tuple.39), branch_computations={%region_4.0_spmd, %region_5.0_spmd} | conditional | flops 4455530496 | bytes 61931632 | solution.py:60
  167.8 2.6 %broadcast.24 = f32[768,1536]{0,1:T(8,128)} broadcast(f32[]{:T(128)} %constant.3.clone), dimensions={} | broadcast | bytes 4718596 | tf_op jit(solution)/shard_map/broadcast.4
  170.3 6.1 %copy.26 = f32[768,1536]{1,0:T(8,128)} copy(f32[768,1536]{0,1:T(8,128)} %get-tuple-element.58) | data formatting | bytes 9437184
  176.5 0.0 reduce-scatter.9.cloned.1.call-update
  176.5 0.0 reduce-scatter.7.cloned.1.call-done
  176.5 1.3 fusion
  177.9 0.3 copy.28
  178.1 0.3 copy.29
  178.4 0.1 mul.32
  178.5 0.2 copy.18
  178.8 3.0 %reshape.44 = f32[12,16,48,16]{3,2,1,0:T(8,128)} reshape(f32[192,768]{1,0:T(8,128)S(1)} %copy.18) | data formatting | bytes 1179648 | tf_op jit(solution)/shard_map/reshape | solution.py:73
  181.7 2.7 %reduce_sum.18 = f32[12,48]{1,0:T(8,128)S(1)} reduce(f32[12,16,48,16]{3,2,1,0:T(8,128)} %reshape.44, f32[]{:T(128)} %constant.10.clone.1), dimensions={1,3}, to_apply=%region_3.0 | reduce | flops 146880 | bytes 592132 | tf_op jit(solution)/shard_map/reduce_sum | solution.py:76
  184.5 54.6 %reduce-scatter.9.cloned.1.call-done = f32[192,1536]{1,0:T(8,128)} async-done(((f32[768,1536]{1,0:T(8,128)}), f32[192,1536]{1,0:T(8,128)}) %reduce-scatter.9.cloned.1.call-update) | async-done | bytes 1179664
  239.1 1.3 fusion.1
  240.4 0.3 copy.30
  240.7 0.3 copy.31
  241.0 0.1 mul.35
  241.1 0.2 copy.20
  241.3 3.0 %reshape.45 = f32[12,16,48,16]{3,2,1,0:T(8,128)} reshape(f32[192,768]{1,0:T(8,128)S(1)} %copy.20) | data formatting | bytes 1179648 | tf_op jit(solution)/shard_map/reshape | solution.py:73
  244.3 2.7 %reduce_sum.19 = f32[12,48]{1,0:T(8,128)S(1)} reduce(f32[12,16,48,16]{3,2,1,0:T(8,128)} %reshape.45, f32[]{:T(128)} %constant.10.clone.1), dimensions={1,3}, to_apply=%region_7.0 | reduce | flops 146880 | bytes 592132 | tf_op jit(solution)/shard_map/reduce_sum | solution.py:76
  247.0 0.6 maximum_bitcast_fusion
  (4 shorter events, 0.0 us)
Async XLA Ops:
  6.5 170.0 %reduce-scatter.7.cloned.1.call-start = ((), (), s32[]{:S(2)}) async-start(), calls=%async_computation.2 | async-start | bytes 5898240
  6.5 6.7 %copy-start.4 = (bf16[48,16,1024]{2,1,0:T(8,128)(2,1)S(1)}, bf16[48,16,1024]{2,1,0:T(8,128)(2,1)}, u32[]{:S(2)}) copy-start(bf16[48,16,1024]{2,1,0:T(8,128)(2,1)} %param.8) | copy-start | bytes 4718596
  6.5 8.3 %copy-start = (s32[1,2]{1,0:T(1,128)S(1)}, s32[1,2]{1,0:T(1,128)}, u32[]{:S(2)}) copy-start(s32[1,2]{1,0:T(1,128)} %param.9) | copy-start | bytes 28
  13.2 71.4 %collective-permute-start = (bf16[768,2752]{0,1:T(8,128)(2,1)}, bf16[768,2752]{0,1:T(8,128)(2,1)S(1)}, u32[]{:S(2)}, u32[]{:S(2)}) collective-permute-start(bf16[768,2752]{0,1:T(8,128)(2,1)} %copy.16), channel_id=1, source_target_pairs={{0,4},{4,8},{8,12},{12,16},{16,20},{20,24},{24,28},{28,32},{32,36}... | collective-permute-start | bytes 12681224 | tf_op jit(solution)/shard_map/ppermute | solution.py:16
  13.2 71.3 %collective-permute-start.1 = (bf16[768,1024]{1,0:T(8,128)(2,1)S(1)}, bf16[768,1024]{1,0:T(8,128)(2,1)S(1)}, u32[]{:S(2)}, u32[]{:S(2)}) collective-permute-start(bf16[768,1024]{1,0:T(8,128)(2,1)S(1)} %bitcast.25), channel_id=1, source_target_pairs={{0,4},{4,8},{8,12},{12,16},{16,20},{20,24},{24,28},{28,32},{32,36}... | collective-permute-start | bytes 4718600 | tf_op jit(solution)/shard_map/ppermute | solution.py:16
  84.5 2.1 copy-start.1
  95.2 143.9 %reduce-scatter.9.cloned.1.call-start = ((), (), s32[]{:S(2)}) async-start(), calls=%async_computation.3 | async-start | bytes 5898240
  95.3 72.5 %collective-permute-start.2 = (bf16[768,2752]{0,1:T(8,128)(2,1)}, bf16[768,2752]{0,1:T(8,128)(2,1)S(1)}, u32[]{:S(2)}, u32[]{:S(2)}) collective-permute-start(bf16[768,2752]{0,1:T(8,128)(2,1)} %copy-done.1), channel_id=1, source_target_pairs={{0,4},{4,8},{8,12},{12,16},{16,20},{20,24},{24,28},{28,32},{32,36}... | collective-permute-start | bytes 12681224 | tf_op jit(solution)/shard_map/ppermute | solution.py:16
  95.4 72.4 %collective-permute-start.3 = (bf16[768,1024]{1,0:T(8,128)(2,1)S(1)}, bf16[768,1024]{1,0:T(8,128)(2,1)S(1)}, u32[]{:S(2)}, u32[]{:S(2)}) collective-permute-start(bf16[768,1024]{1,0:T(8,128)(2,1)S(1)} %collective-permute-done.1), channel_id=1, source_target_pairs={{0,4},{4,8},{8,12},{12,16},{16,20},{20,24},{24,28},{28,32},{32,36}... | collective-permute-start | bytes 4718600 | tf_op jit(solution)/shard_map/ppermute | solution.py:16
Sparse Core Ops, SparseCore 0:
  95.4 58.7 reduce-scatter.6
  176.6 62.4 reduce-scatter.8
where the time goes:
time: 258 us; the launch traced here: 254 us
  waiting for transfers between devices  195 us (76%)
  local copies, waits for them, and re-layouts  36.7 us (14%)
  between operations  14.7 us (6%)
  other arithmetic  6.28 us (2%)
    ppermute x4, waiting for transfers between devices, from_behind(): return lax.ppermute(value, axis, pairs)  140 us
    unnamed x4, waiting for transfers between devices  54.7 us
    unnamed x12, local copies, waits for them, and re-layouts  15.4 us
    reshape x1, local copies, waits for them, and re-layouts, per_device(): hidden.reshape(block_rows, hidden_width)  6.65 us
    reshape x2, local copies, waits for them, and re-layouts, per_device(): (left_gram * right_gram).reshape(summed.shape[0] // tokens, tokens, sampl...  5.95 us
    reduce_sum x2, other arithmetic, per_device(): kernel_tiles.append(jnp.sum(product, axis=(1, 3)) * kernel_scale)  5.44 us
  transfers between devices with their start and end apart: 6, of which 3 were waited for; matrix products, arithmetic and copies ran while one was open for 7% of the time, Pallas kernels for 0%

commit v1 on v0

v1 whole, which is shorter than its diff:
```python
import functools
import math

import jax
import jax.numpy as jnp
from jax import lax
from jax.experimental import pallas as pl
from jax.experimental.pallas import tpu as pltpu
from jax.sharding import PartitionSpec as P

D = 4096
FF = 11008
CHUNKS = 6
PARTS = 4
LANES = 128
NEAR, FAR = 0, 1
LEFT, RIGHT = 0, 1


def contract(rows, columns):
    return lax.dot_general(
        rows, columns, (((1,), (1,)), ((), ())), preferred_element_type=jnp.float32
    )


def exact_dot(a, b):
    return jnp.dot(
        a, b, precision=lax.Precision.HIGHEST, preferred_element_type=jnp.float32
    )


def tile_kernel(
    grid_rows,
    grid_cols,
    hidden_ref,
    cotan_ref,
    out_ref,
    own_hidden,
    own_cotan,
    got_hidden,
    got_cotan,
    gram,
    relay_in,
    direct_in,
    passed,
    passed_in,
    row_sums,
    lane_pick,
    keep,
    row_pick,
    result,
    landed,
    load_sem,
    far_send,
    near_send,
    got_sem,
    first_send,
    relay_recv,
    direct_recv,
    pass_send,
    pass_recv,
    result_send,
    result_recv,
):
    row = lax.axis_index("row")
    col = lax.axis_index("col")
    me = lax.axis_index("tensor")
    core = lax.rem(col, 2)
    units = 2 * CHUNKS
    block_rows = own_hidden.shape[0]
    quarter = block_rows // PARTS
    piece = quarter // CHUNKS
    width = hidden_ref.shape[-1]
    cotan_width = cotan_ref.shape[-1]

    up = lax.rem(me + 1, PARTS)
    down = lax.rem(me + PARTS - 1, PARTS)
    across = lax.rem(me + 2, PARTS)
    up_id = (row, col, up)
    down_id = (row, col, down)
    partner_id = (row, col + 1 - 2 * core, me)
    next_id = (
        lax.rem(row + (col + 2) // grid_cols, grid_rows),
        lax.rem(col + 2, grid_cols),
        me,
    )
    prev_id = (
        lax.rem(row + grid_rows - 1 + (col + grid_cols - 2) // grid_cols, grid_rows),
        lax.rem(col + grid_cols - 2, grid_cols),
        me,
    )
    even = core == 0
    far_id = tuple(jnp.where(even, p, n) for p, n in zip(prev_id, next_id))

    loads = (
        pltpu.make_async_copy(hidden_ref, own_hidden_view(own_hidden, piece), load_sem.at[0]),
        pltpu.make_async_copy(cotan_ref, own_hidden_view(own_cotan, piece), load_sem.at[1]),
    )
    for load in loads:
        load.start()

    barrier = pltpu.get_barrier_semaphore()
    peers = (up_id, down_id, partner_id, next_id, prev_id)
    for peer in peers:
        pl.semaphore_signal(
            barrier, inc=1, device_id=peer, device_id_type=pl.DeviceIdType.MESH
        )
    pl.semaphore_wait(barrier, len(peers))

    def send(source, target, send_sem, recv_sem, device):
        return pltpu.make_async_remote_copy(
            src_ref=source,
            dst_ref=target,
            send_sem=send_sem,
            recv_sem=recv_sem,
            device_id=device,
            device_id_type=pl.DeviceIdType.MESH,
        )

    def far_copies(k):
        slot = FAR * CHUNKS + k
        return (
            send(hidden_ref.at[:, k], got_hidden.at[slot], far_send.at[k, 0], got_sem.at[slot, 0], far_id),
            send(cotan_ref.at[:, k], got_cotan.at[slot], far_send.at[k, 1], got_sem.at[slot, 1], far_id),
        )

    def near_copies_own(k):
        return (
            send(hidden_ref.at[:, k], got_hidden.at[k], near_send.at[k, 0], got_sem.at[k, 0], partner_id),
            send(cotan_ref.at[:, k], got_cotan.at[k], near_send.at[k, 1], got_sem.at[k, 1], partner_id),
        )

    def near_copies_on(k):
        slot = FAR * CHUNKS + k
        return (
            send(got_hidden.at[slot], got_hidden.at[k], near_send.at[k, 0], got_sem.at[k, 0], partner_id),
            send(got_cotan.at[slot], got_cotan.at[k], near_send.at[k, 1], got_sem.at[k, 1], partner_id),
        )

    @pl.loop(0, CHUNKS)
    def _(k):
        for copy in far_copies(k):
            copy.start()

        @pl.when(even)
        def _():
            for copy in near_copies_own(k):
                copy.start()

    def unit_of(n):
        lead = CHUNKS // 2
        later = n - lead
        even_stream = jnp.where(lax.rem(n, 2) == 0, FAR, NEAR)
        mixed = lax.rem(later, 2) == 0
        odd_stream = jnp.where(
            n < lead, NEAR, jnp.where(later < CHUNKS, jnp.where(mixed, FAR, NEAR), FAR)
        )
        odd_chunk = jnp.where(
            n < lead,
            n,
            jnp.where(
                later < CHUNKS,
                jnp.where(mixed, later // 2, lead + later // 2),
                later - lead,
            ),
        )
        return (
            jnp.where(even, even_stream, odd_stream),
            jnp.where(even, n // 2, odd_chunk),
        )

    def relayed_after(n):
        lead = CHUNKS // 2
        paired = jnp.where(lax.rem(n, 2) == 0, n, n + 1)
        crossed = jnp.where(lax.rem(n, 2) == 0, n + 1, n)
        odd_count = jnp.where(
            n < lead, n, jnp.where(n < lead + CHUNKS, crossed, n + 1)
        )
        return jnp.where(even, paired, odd_count)

    def first_copies(n):
        return (
            send(gram.at[n, LEFT, across], relay_in.at[n, LEFT], first_send.at[n, 0], relay_recv.at[n, LEFT], up_id),
            send(gram.at[n, RIGHT, across], relay_in.at[n, RIGHT], first_send.at[n, 1], relay_recv.at[n, RIGHT], down_id),
            send(gram.at[n, RIGHT, up], direct_in.at[n, RIGHT], first_send.at[n, 2], direct_recv.at[n, RIGHT], up_id),
            send(gram.at[n, LEFT, down], direct_in.at[n, LEFT], first_send.at[n, 3], direct_recv.at[n, LEFT], down_id),
        )

    def pass_copies(n):
        return (
            send(passed.at[n, LEFT], passed_in.at[n, LEFT], pass_send.at[n, LEFT], pass_recv.at[n, LEFT], up_id),
            send(passed.at[n, RIGHT], passed_in.at[n, RIGHT], pass_send.at[n, RIGHT], pass_recv.at[n, RIGHT], down_id),
        )

    def compute(n, stream, k):
        slot = stream * CHUNKS + k
        natural = jnp.logical_and(even, stream == FAR)

        def grams(own, got, which):
            chunk = got[slot].reshape(PARTS * piece, got.shape[-1])

            @pl.when(natural)
            def _():
                for part in range(PARTS):
                    gram[n, which, part] = contract(
                        own[part * quarter : (part + 1) * quarter, :], chunk
                    )

            @pl.when(jnp.logical_not(natural))
            def _():
                wide = 2 * LANES
                for block in range(block_rows // wide):
                    value = contract(chunk, own[block * wide : (block + 1) * wide, :])
                    for part in range(PARTS):
                        for half in range(2):
                            start = (2 * block + half) * piece
                            gram[n, which, part, start : start + piece, :] = value[
                                part * piece : (part + 1) * piece,
                                half * LANES : (half + 1) * LANES,
                            ]

        grams(own_hidden, got_hidden, LEFT)
        grams(own_cotan, got_cotan, RIGHT)

    def relay(n):
        copies, onward = first_copies(n), pass_copies(n)
        copies[0].wait_recv()
        passed[n, LEFT] = relay_in[n, LEFT] + gram[n, LEFT, up]
        onward[0].start()
        copies[1].wait_recv()
        passed[n, RIGHT] = relay_in[n, RIGHT] + gram[n, RIGHT, down]
        onward[1].start()

    def finish(n):
        stream, k = unit_of(n)
        copies, onward = first_copies(n), pass_copies(n)
        copies[2].wait_recv()
        copies[3].wait_recv()
        onward[0].wait_recv()
        onward[1].wait_recv()
        left = gram[n, LEFT, me] + passed_in[n, LEFT] + direct_in[n, LEFT]
        right = gram[n, RIGHT, me] + passed_in[n, RIGHT] + direct_in[n, RIGHT]
        product = left * right
        tokens = 16
        row_sums[stream * CHUNKS + k, : quarter // tokens, :] = jnp.sum(
            product.reshape(quarter // tokens, tokens, LANES), axis=1
        )

    row_sums[...] = jnp.zeros_like(row_sums)
    build_picks(even, lane_pick, keep, row_pick)
    for load in loads:
        load.wait()

    @pl.loop(0, units)
    def _(n):
        stream, k = unit_of(n)
        slot = stream * CHUNKS + k
        send(hidden_ref.at[:, k], got_hidden.at[slot], far_send.at[k, 0], got_sem.at[slot, 0], far_id).wait_recv()
        send(cotan_ref.at[:, k], got_cotan.at[slot], far_send.at[k, 1], got_sem.at[slot, 1], far_id).wait_recv()

        @pl.when(jnp.logical_and(jnp.logical_not(even), stream == FAR))
        def _():
            for copy in near_copies_on(k):
                copy.start()

        compute(n, stream, k)
        for copy in first_copies(n):
            copy.start()

        @pl.loop(jnp.where(n > 0, relayed_after(n - 1), 0), relayed_after(n))
        def _(m):
            relay(m)

        @pl.when(n >= 2)
        def _():
            finish(n - 2)

    def epilogue(stream):
        sums = row_sums[pl.ds(stream * CHUNKS, CHUNKS)].reshape(CHUNKS * 16, LANES)
        spread = exact_dot(sums, lane_pick[stream]) * keep[stream]
        result[stream] = exact_dot(row_pick[stream], spread)

    result_copy = send(result.at[FAR], landed, result_send, result_recv, next_id)
    finish(units - 2)
    epilogue(jnp.where(even, FAR, NEAR))

    @pl.when(even)
    def _():
        result_copy.start()

    finish(units - 1)
    epilogue(jnp.where(even, NEAR, FAR))
    out_ref[0] = result[NEAR]

    @pl.when(even)
    def _():
        result_copy.wait()
        out_ref[1] = landed[...]

    @pl.when(jnp.logical_not(even))
    def _():
        out_ref[1] = result[FAR]

    @pl.loop(0, CHUNKS)
    def _(k):
        for copy in far_copies(k):
            copy.wait_send()
        for copy in near_copies_own(k):
            copy.wait_send()

    @pl.loop(0, units)
    def _(n):
        for copy in first_copies(n):
            copy.wait_send()
        for copy in pass_copies(n):
            copy.wait_send()


def own_hidden_view(own, piece):
    return own.reshape(PARTS, CHUNKS, piece, own.shape[-1])


def build_picks(even, lane_pick, keep, row_pick):
    def iota(shape, axis):
        return lax.broadcasted_iota(jnp.int32, shape, axis)

    def twelfth(j):
        return (
            (j >= 12).astype(jnp.int32)
            + (j >= 24).astype(jnp.int32)
            + (j >= 36).astype(jnp.int32)
        )

    held = CHUNKS * 16
    lane, target = iota((LANES, LANES), 0), iota((LANES, LANES), 1)
    group = lane >> 4
    own = jnp.logical_and(group == (target & 7), target < 48).astype(jnp.float32)
    other = jnp.logical_and(
        group == 2 * twelfth(target) + (target & 1), target < 48
    ).astype(jnp.float32)
    line, target = iota((held, LANES), 0), iota((held, LANES), 1)
    own_keep = (((line & 15) >> 1) == (target >> 3)).astype(jnp.float32)
    other_keep = (
        (line >> 4) == ((target - 12 * twelfth(target)) >> 1)
    ).astype(jnp.float32)
    out, line = iota((16, held), 0), iota((16, held), 1)
    place = line & 15
    own_row = jnp.logical_and(
        2 * (line >> 4) + (place & 1) == out, place < 12
    ).astype(jnp.float32)
    other_row = jnp.logical_and(place == out, place < 12).astype(jnp.float32)
    lane_pick[NEAR] = own
    keep[NEAR] = own_keep
    row_pick[NEAR] = own_row
    lane_pick[FAR] = jnp.where(even, other, own)
    keep[FAR] = jnp.where(even, other_keep, own_keep)
    row_pick[FAR] = jnp.where(even, other_row, own_row)


def solution(mesh):
    grid_rows, grid_cols = mesh.shape["row"], mesh.shape["col"]
    placed = (
        P(("row", "col"), None, "tensor"),
        P(("row", "col"), None, "tensor"),
        P(("row", "col"), None),
    )

    def per_device(hidden, cotangent, tile_live):
        samples, tokens, width = hidden.shape
        cotan_width = cotangent.shape[2]
        block_rows = samples * tokens
        quarter = block_rows // PARTS
        piece = quarter // CHUNKS
        units = 2 * CHUNKS
        f32, bf16 = jnp.float32, jnp.bfloat16
        vmem, dma = pltpu.VMEM, pltpu.SemaphoreType.DMA
        held = pltpu.MemorySpace.HBM
        part = (quarter, LANES)
        sums = pl.pallas_call(
            functools.partial(tile_kernel, grid_rows, grid_cols),
            out_shape=jax.ShapeDtypeStruct((2, 16, LANES), f32),
            in_specs=[pl.BlockSpec(memory_space=held)] * 2,
            out_specs=pl.BlockSpec(memory_space=pltpu.VMEM),
            scratch_shapes=[
                vmem((block_rows, width), bf16),
                vmem((block_rows, cotan_width), bf16),
                vmem((units, PARTS, piece, width), bf16),
                vmem((units, PARTS, piece, cotan_width), bf16),
                vmem((units, 2, PARTS) + part, f32),
                vmem((units, 2) + part, f32),
                vmem((units, 2) + part, f32),
                vmem((units, 2) + part, f32),
                vmem((units, 2) + part, f32),
                vmem((units, 16, LANES), f32),
                vmem((2, LANES, LANES), f32),
                vmem((2, CHUNKS * 16, LANES), f32),
                vmem((2, 16, CHUNKS * 16), f32),
                vmem((2, 16, LANES), f32),
                vmem((16, LANES), f32),
                dma((2,)),
                dma((CHUNKS, 2)),
                dma((CHUNKS, 2)),
                dma((units, 2)),
                dma((units, 4)),
                dma((units, 2)),
                dma((units, 2)),
                dma((units, 2)),
                dma((units, 2)),
                dma,
                dma,
            ],
            compiler_params=pltpu.CompilerParams(
                collective_id=0,
                has_side_effects=True,
                vmem_limit_bytes=60 * 1024 * 1024,
            ),
        )(
            hidden.reshape(PARTS, CHUNKS, piece, width),
            cotangent.reshape(PARTS, CHUNKS, piece, cotan_width),
        )
        kernel_scale = 1.0 / (tokens * math.sqrt(FF * D))
        live = tile_live[0].astype(f32)[:, None, None] * kernel_scale
        return (sums[:, : samples // PARTS, :samples] * live)[None]

    return jax.shard_map(
        per_device,
        mesh=mesh,
        in_specs=placed,
        out_specs=P(("row", "col"), None, "tensor", None),
        check_vma=False,
    )
```

time: 258 us -> 103 us (0.40); the launches traced: 254 us -> 103 us
  waiting for transfers between devices: 195 us -> 0 us
  Pallas kernels: 0 us -> 101 us
  local copies, waits for them, and re-layouts: 36.7 us -> 0.61 us
  between operations: 14.7 us -> 0.01 us
  other arithmetic: 6.28 us -> 1.45 us
    ppermute x4 -> x0, waiting for transfers between devices: 140 us -> none  [from_behind(): return lax.ppermute(value, axis, pairs)]
    pallas_call x0 -> x1, Pallas kernels: none -> 101 us  [per_device(): pl.pallas_call(functools.partial(tile_kernel, grid_rows, grid_cols), out_...]
    unnamed x4 -> x0, waiting for transfers between devices: 54.7 us -> none
    unnamed x12 -> x0, local copies, waits for them, and re-layouts: 15.4 us -> none
    reshape x3 -> x0, local copies, waits for them, and re-layouts: 12.6 us -> none  [the longest x1 6.65 us: per_device(): hidden.reshape(block_rows, hidden_width)]
    reduce_sum x2 -> x0, other arithmetic: 5.44 us -> none  [per_device(): kernel_tiles.append(jnp.sum(product, axis=(1, 3)) * kernel_scale)]
    another operation x2 -> x0, local copies, waits for them, and re-layouts: 5.04 us -> none
    slice x3 -> x0, local copies, waits for them, and re-layouts: 3.19 us -> none  [the longest x2 2.64 us: per_device(): right_gram = summed[:, block_rows:]]
  transfers between devices with their start and end apart: 6 -> 0, of which waited for: 3 -> 0; matrix products, arithmetic and copies ran while one was open for 7% -> 0% of each run, Pallas kernels for 0% -> 0%
where the time goes in v1:
time: 103 us
  Pallas kernels  101 us (98%)
  other arithmetic  1.45 us (1%)
    pallas_call x1, Pallas kernels, per_device(): pl.pallas_call(functools.partial(tile_kernel, grid_rows, grid_cols), out_...  101 us

profile of v1, /device:TPU:2, one launch (start us, length us, event | category | flops | bytes accessed | tf_op | source)
XLA Modules:
  0.0 103.3 jit_solution(11826713908790641570)
XLA Ops:
  0.0 0.7 multiply_bitcast_fusion.1
  0.7 101.3 %shard_map.37 = f32[2,16,128]{2,1,0:T(8,128)} custom-call(bf16[4,6,32,2752]{3,2,1,0:T(8,128)(2,1)} %bitcast.6, bf16[4,6,32,1024]{3,2,1,0:T(8,128)(2,1)} %bitcast.7), custom_call_target="tpu_custom_call" | custom-call | tf_op jit(solution)/shard_map/pallas_call | solution.py:379
  101.9 0.8 multiply_bitcast_fusion
  102.7 0.6 copy.4

commit v2 on v1

v2 whole, which is shorter than its diff:
```python
import functools
import math

import jax
import jax.numpy as jnp
from jax import lax
from jax.experimental import pallas as pl
from jax.experimental.pallas import tpu as pltpu
from jax.sharding import PartitionSpec as P

D = 4096
FF = 11008
CHUNKS = 6
PARTS = 4
LANES = 128
TOKENS = 16
NEAR, FAR = 0, 1
UP, DOWN = 0, 1
STEPS = 127.0 * 256.0
LEFT, RIGHT = 0, 1


def contract(rows, columns):
    return lax.dot_general(
        rows, columns, (((1,), (1,)), ((), ())), preferred_element_type=jnp.float32
    )


def exact_dot(a, b):
    return jnp.dot(
        a, b, precision=lax.Precision.HIGHEST, preferred_element_type=jnp.float32
    )


def pack(value, head_ref, rest_ref):
    half = value.shape[0] // 2
    head = value.astype(jnp.bfloat16)
    wide = head.astype(jnp.float32)
    rest = jnp.round((value - wide) * (STEPS / jnp.maximum(jnp.abs(wide), 1e-30)))
    both = rest[:half] * 256.0 + rest[half:]
    head_ref[...] = head
    rest_ref[...] = both.astype(jnp.int32).astype(jnp.int16)


def unpack(head_ref, rest_ref):
    wide = head_ref[...].astype(jnp.float32)
    both = rest_ref[...].astype(jnp.int32).astype(jnp.float32)
    first = jnp.floor((both + 128.0) * (1.0 / 256.0))
    rest = jnp.concatenate([first, both - 256.0 * first], axis=0)
    return wide + jnp.abs(wide) * (rest * (1.0 / STEPS))


def tile_kernel(
    grid_rows,
    grid_cols,
    hidden_ref,
    cotan_ref,
    out_ref,
    own_hidden,
    own_cotan,
    got_hidden,
    got_cotan,
    gram,
    first_head,
    first_rest,
    first_head_in,
    first_rest_in,
    pass_head,
    pass_rest,
    pass_head_in,
    pass_rest_in,
    row_sums,
    lane_pick,
    keep,
    row_pick,
    result,
    landed,
    load_sem,
    block_send,
    got_sem,
    first_send,
    first_recv,
    pass_send,
    pass_recv,
    result_send,
    result_recv,
):
    row = lax.axis_index("row")
    col = lax.axis_index("col")
    me = lax.axis_index("tensor")
    core = lax.rem(col, 2)
    even = core == 0
    odd = core == 1
    units = 2 * CHUNKS
    block_rows = own_hidden.shape[0]
    quarter = block_rows // PARTS
    piece = quarter // CHUNKS

    up = lax.rem(me + 1, PARTS)
    down = lax.rem(me + PARTS - 1, PARTS)
    across = lax.rem(me + 2, PARTS)
    up_id = (row, col, up)
    down_id = (row, col, down)
    partner_id = (row, col + 1 - 2 * core, me)
    next_id = (
        lax.rem(row + (col + 2) // grid_cols, grid_rows),
        lax.rem(col + 2, grid_cols),
        me,
    )
    prev_id = (
        lax.rem(row + grid_rows - 1 + (col + grid_cols - 2) // grid_cols, grid_rows),
        lax.rem(col + grid_cols - 2, grid_cols),
        me,
    )
    far_id = tuple(jnp.where(even, p, n) for p, n in zip(prev_id, next_id))

    def by_piece(own):
        return own.reshape(PARTS, CHUNKS, piece, own.shape[-1])

    loads = (
        pltpu.make_async_copy(hidden_ref, by_piece(own_hidden), load_sem.at[0]),
        pltpu.make_async_copy(cotan_ref, by_piece(own_cotan), load_sem.at[1]),
    )
    for load in loads:
        load.start()

    barrier = pltpu.get_barrier_semaphore()
    peers = (up_id, down_id, partner_id, next_id, prev_id)
    for peer in peers:
        pl.semaphore_signal(
            barrier, inc=1, device_id=peer, device_id_type=pl.DeviceIdType.MESH
        )
    pl.semaphore_wait(barrier, len(peers))

    def send(source, target, send_sem, recv_sem, device):
        return pltpu.make_async_remote_copy(
            src_ref=source,
            dst_ref=target,
            send_sem=send_sem,
            recv_sem=recv_sem,
            device_id=device,
            device_id_type=pl.DeviceIdType.MESH,
        )

    def block_copies(stream, k, device):
        return tuple(
            send(
                source.at[:, k],
                target.at[stream, :, k],
                block_send.at[stream, k, which],
                got_sem.at[stream, k, which],
                device,
            )
            for which, (source, target) in enumerate(
                ((hidden_ref, got_hidden), (cotan_ref, got_cotan))
            )
        )

    @pl.loop(0, CHUNKS)
    def _(k):
        for copy in block_copies(FAR, k, far_id):
            copy.start()
        for copy in block_copies(NEAR, k, partner_id):
            copy.start()

    def wait_block(stream, k):
        for copy in block_copies(stream, k, partner_id):
            copy.wait_recv()

    def unit_of(n):
        return (
            jnp.where(even, n // CHUNKS, lax.rem(n, 2)),
            jnp.where(even, lax.rem(n, CHUNKS), n // 2),
        )

    def relayed_after(n):
        late = jnp.where(n < CHUNKS + 2, n, n + 1)
        paired = jnp.where(lax.rem(n, 2) == 0, n, n + 1)
        return jnp.where(even, late, paired)

    def first_copies(n, way):
        device = (up_id, down_id)[way]
        return (
            send(first_head.at[n, way], first_head_in.at[n, way], first_send.at[n, way, 0], first_recv.at[n, way, 0], device),
            send(first_rest.at[n, way], first_rest_in.at[n, way], first_send.at[n, way, 1], first_recv.at[n, way, 1], device),
        )

    def pass_copies(n, way):
        device = (up_id, down_id)[way]
        return (
            send(pass_head.at[n, way], pass_head_in.at[n, way], pass_send.at[n, way, 0], pass_recv.at[n, way, 0], device),
            send(pass_rest.at[n, way], pass_rest_in.at[n, way], pass_send.at[n, way, 1], pass_recv.at[n, way, 1], device),
        )

    def rows_first(n, which, own, chunk):
        wide = 2 * LANES
        for block in range(block_rows // wide):
            value = contract(chunk, own[block * wide : (block + 1) * wide, :])
            for part in range(PARTS):
                for half in range(2):
                    start = (2 * block + half) * piece
                    gram[n, which, part, start : start + piece, :] = value[
                        part * piece : (part + 1) * piece,
                        half * LANES : (half + 1) * LANES,
                    ]

    def compute(n, tile, k):
        def chunk_of(got, stream):
            return got[stream, :, k].reshape(PARTS * piece, got.shape[-1])

        pairs = ((own_hidden, got_hidden), (own_cotan, got_cotan))

        @pl.when(even)
        def _():
            for which, (own, got) in enumerate(pairs):
                chunk = chunk_of(got, tile)
                for part in range(PARTS):
                    gram[n, which, part] = contract(
                        own[part * quarter : (part + 1) * quarter, :], chunk
                    )

        @pl.when(jnp.logical_and(odd, tile == 0))
        def _():
            for which, (_, got) in enumerate(pairs):
                other = got.at[NEAR].reshape(block_rows, got.shape[-1])
                rows_first(n, which, other, chunk_of(got, FAR))

        @pl.when(jnp.logical_and(odd, tile == 1))
        def _():
            for which, (own, got) in enumerate(pairs):
                rows_first(n, which, own, chunk_of(got, FAR))

        pack(gram[n, LEFT, across], first_head.at[n, UP, 0], first_rest.at[n, UP, 0])
        pack(gram[n, RIGHT, up], first_head.at[n, UP, 1], first_rest.at[n, UP, 1])
        pack(gram[n, RIGHT, across], first_head.at[n, DOWN, 0], first_rest.at[n, DOWN, 0])
        pack(gram[n, LEFT, down], first_head.at[n, DOWN, 1], first_rest.at[n, DOWN, 1])
        for way in (UP, DOWN):
            for copy in first_copies(n, way):
                copy.start()

    def relay(n):
        for way, which, onward in ((UP, LEFT, up), (DOWN, RIGHT, down)):
            for copy in first_copies(n, way):
                copy.wait_recv()
            total = gram[n, which, onward] + unpack(
                first_head_in.at[n, way, 0], first_rest_in.at[n, way, 0]
            )
            pack(total, pass_head.at[n, way], pass_rest.at[n, way])
            for copy in pass_copies(n, way):
                copy.start()

    def finish(n):
        tile, k = unit_of(n)
        for way in (UP, DOWN):
            for copy in pass_copies(n, way):
                copy.wait_recv()
        left, right = (
            gram[n, which, me]
            + unpack(pass_head_in.at[n, way], pass_rest_in.at[n, way])
            + unpack(first_head_in.at[n, 1 - way, 1], first_rest_in.at[n, 1 - way, 1])
            for which, way in ((LEFT, UP), (RIGHT, DOWN))
        )
        row_sums[tile * CHUNKS + k, : quarter // TOKENS, :] = jnp.sum(
            (left * right).reshape(quarter // TOKENS, TOKENS, LANES), axis=1
        )

    def epilogue(tile):
        sums = row_sums[pl.ds(tile * CHUNKS, CHUNKS)].reshape(CHUNKS * TOKENS, LANES)
        result[tile] = exact_dot(row_pick[...], exact_dot(sums, lane_pick[...]) * keep[...])

    swapped = send(result.at[0], landed.at[0], result_send.at[0], result_recv.at[0], partner_id)
    moved = send(result.at[1], landed.at[1], result_send.at[1], result_recv.at[1], next_id)

    row_sums[...] = jnp.zeros_like(row_sums)
    build_picks(even, lane_pick, keep, row_pick)
    for load in loads:
        load.wait()

    @pl.when(odd)
    def _():
        @pl.loop(0, CHUNKS)
        def _(k):
            wait_block(NEAR, k)

    @pl.loop(0, units)
    def _(n):
        tile, k = unit_of(n)

        @pl.when(jnp.logical_or(even, tile == 0))
        def _():
            wait_block(jnp.where(even, tile, FAR), k)

        compute(n, tile, k)

        @pl.loop(jnp.where(n > 0, relayed_after(n - 1), 0), relayed_after(n))
        def _(m):
            relay(m)

        @pl.when(n >= 2)
        def _():
            finish(n - 2)

        @pl.when(jnp.logical_and(even, n == CHUNKS + 2))
        def _():
            epilogue(0)
            swapped.start()

    finish(units - 2)

    @pl.when(odd)
    def _():
        epilogue(0)
        swapped.start()

    finish(units - 1)
    epilogue(1)

    @pl.when(even)
    def _():
        moved.start()

    @pl.loop(0, CHUNKS)
    def _(k):
        for stream in (NEAR, FAR):
            for copy in block_copies(stream, k, partner_id):
                copy.wait_send()

    @pl.loop(0, units)
    def _(n):
        for way in (UP, DOWN):
            for copy in first_copies(n, way):
                copy.wait_send()
            for copy in pass_copies(n, way):
                copy.wait_send()

    swapped.wait()
    out_ref[0] = landed[0]

    @pl.when(even)
    def _():
        moved.wait()
        out_ref[1] = landed[1]

    @pl.when(odd)
    def _():
        out_ref[1] = result[1]


def build_picks(even, lane_pick, keep, row_pick):
    def iota(shape, axis):
        return lax.broadcasted_iota(jnp.int32, shape, axis)

    def twelfth(j):
        return (
            (j >= 12).astype(jnp.int32)
            + (j >= 24).astype(jnp.int32)
            + (j >= 36).astype(jnp.int32)
        )

    held = CHUNKS * TOKENS
    lane, target = iota((LANES, LANES), 0), iota((LANES, LANES), 1)
    group = lane >> 4
    by_rows = jnp.logical_and(group == (target & 7), target < 48).astype(jnp.float32)
    by_lanes = jnp.logical_and(
        group == 2 * twelfth(target) + (target & 1), target < 48
    ).astype(jnp.float32)
    lane_pick[...] = jnp.where(even, by_lanes, by_rows)
    line, target = iota((held, LANES), 0), iota((held, LANES), 1)
    by_rows = (((line & 15) >> 1) == (target >> 3)).astype(jnp.float32)
    by_lanes = (
        (line >> 4) == ((target - 12 * twelfth(target)) >> 1)
    ).astype(jnp.float32)
    keep[...] = jnp.where(even, by_lanes, by_rows)
    out, line = iota((16, held), 0), iota((16, held), 1)
    place = line & 15
    by_rows = jnp.logical_and(
        2 * (line >> 4) + (place & 1) == out, place < 12
    ).astype(jnp.float32)
    by_lanes = jnp.logical_and(place == out, place < 12).astype(jnp.float32)
    row_pick[...] = jnp.where(even, by_lanes, by_rows)


def solution(mesh):
    grid_rows, grid_cols = mesh.shape["row"], mesh.shape["col"]
    placed = (
        P(("row", "col"), None, "tensor"),
        P(("row", "col"), None, "tensor"),
        P(("row", "col"), None),
    )

    def per_device(hidden, cotangent, tile_live):
        samples, tokens, width = hidden.shape
        cotan_width = cotangent.shape[2]
        block_rows = samples * tokens
        quarter = block_rows // PARTS
        piece = quarter // CHUNKS
        units = 2 * CHUNKS
        f32, bf16, i16 = jnp.float32, jnp.bfloat16, jnp.int16
        vmem, dma = pltpu.VMEM, pltpu.SemaphoreType.DMA
        held = pltpu.MemorySpace.HBM
        sums = pl.pallas_call(
            functools.partial(tile_kernel, grid_rows, grid_cols),
            out_shape=jax.ShapeDtypeStruct((2, 16, LANES), f32),
            in_specs=[pl.BlockSpec(memory_space=held)] * 2,
            out_specs=pl.BlockSpec(memory_space=pltpu.VMEM),
            scratch_shapes=[
                vmem((block_rows, width), bf16),
                vmem((block_rows, cotan_width), bf16),
                vmem((2, PARTS, CHUNKS, piece, width), bf16),
                vmem((2, PARTS, CHUNKS, piece, cotan_width), bf16),
                vmem((units, 2, PARTS, quarter, LANES), f32),
                vmem((units, 2, 2, quarter, LANES), bf16),
                vmem((units, 2, 2, quarter // 2, LANES), i16),
                vmem((units, 2, 2, quarter, LANES), bf16),
                vmem((units, 2, 2, quarter // 2, LANES), i16),
                vmem((units, 2, quarter, LANES), bf16),
                vmem((units, 2, quarter // 2, LANES), i16),
                vmem((units, 2, quarter, LANES), bf16),
                vmem((units, 2, quarter // 2, LANES), i16),
                vmem((units, TOKENS, LANES), f32),
                vmem((LANES, LANES), f32),
                vmem((CHUNKS * TOKENS, LANES), f32),
                vmem((TOKENS, CHUNKS * TOKENS), f32),
                vmem((2, TOKENS, LANES), f32),
                vmem((2, TOKENS, LANES), f32),
                dma((2,)),
                dma((2, CHUNKS, 2)),
                dma((2, CHUNKS, 2)),
                dma((units, 2, 2)),
                dma((units, 2, 2)),
                dma((units, 2, 2)),
                dma((units, 2, 2)),
                dma((2,)),
                dma((2,)),
            ],
            compiler_params=pltpu.CompilerParams(
                collective_id=0,
                has_side_effects=True,
                vmem_limit_bytes=60 * 1024 * 1024,
            ),
        )(
            hidden.reshape(PARTS, CHUNKS, piece, width),
            cotangent.reshape(PARTS, CHUNKS, piece, cotan_width),
        )
        kernel_scale = 1.0 / (tokens * math.sqrt(FF * D))
        live = tile_live[0].astype(f32)[:, None, None] * kernel_scale
        return (sums[:, : samples // PARTS, :samples] * live)[None]

    return jax.shard_map(
        per_device,
        mesh=mesh,
        in_specs=placed,
        out_specs=P(("row", "col"), None, "tensor", None),
        check_vma=False,
    )
```

time: 103 us -> 97.4 us (0.946)
  Pallas kernels: 101 us -> 95.1 us
    pallas_call x1, Pallas kernels: 101 us -> 95.1 us  [per_device(): pl.pallas_call(functools.partial(tile_kernel, grid_rows, grid_cols), out_...]
where the time goes in v2:
time: 97.4 us; the launch traced here: 97.2 us
  Pallas kernels  95.1 us (98%)
  other arithmetic  1.45 us (1%)
    pallas_call x1, Pallas kernels, per_device(): pl.pallas_call(functools.partial(tile_kernel, grid_rows, grid_cols), out_...  95.1 us

profile of v2, /device:TPU:2, one launch (start us, length us, event | category | flops | bytes accessed | tf_op | source)
XLA Modules:
  0.0 97.2 jit_solution(8420030929637619144)
XLA Ops:
  0.0 0.7 multiply_bitcast_fusion.1
  0.7 95.1 %shard_map.37 = f32[2,16,128]{2,1,0:T(8,128)} custom-call(bf16[4,6,32,2752]{3,2,1,0:T(8,128)(2,1)} %bitcast.6, bf16[4,6,32,1024]{3,2,1,0:T(8,128)(2,1)} %bitcast.7), custom_call_target="tpu_custom_call" | custom-call | tf_op jit(solution)/shard_map/pallas_call | solution.py:401
  95.8 0.8 multiply_bitcast_fusion
  96.6 0.6 copy.4

commit v3 on v2

--- a/solution.py
+++ b/solution.py
@@ -15,7 +15,7 @@
 LANES = 128
 TOKENS = 16
 NEAR, FAR = 0, 1
-UP, DOWN = 0, 1
+RELAY, DIRECT = 0, 1
 STEPS = 127.0 * 256.0
 LEFT, RIGHT = 0, 1
 
@@ -101,6 +101,7 @@
     across = lax.rem(me + 2, PARTS)
     up_id = (row, col, up)
     down_id = (row, col, down)
+    across_id = (row, col, across)
     partner_id = (row, col + 1 - 2 * core, me)
     next_id = (
         lax.rem(row + (col + 2) // grid_cols, grid_rows),
@@ -125,7 +126,7 @@
         load.start()
 
     barrier = pltpu.get_barrier_semaphore()
-    peers = (up_id, down_id, partner_id, next_id, prev_id)
+    peers = (up_id, down_id, across_id, partner_id, next_id, prev_id)
     for peer in peers:
         pl.semaphore_signal(
             barrier, inc=1, device_id=peer, device_id_type=pl.DeviceIdType.MESH
@@ -142,127 +143,126 @@
             device_id_type=pl.DeviceIdType.MESH,
         )
 
-    def block_copies(stream, k, device):
-        return tuple(
-            send(
-                source.at[:, k],
-                target.at[stream, :, k],
-                block_send.at[stream, k, which],
-                got_sem.at[stream, k, which],
-                device,
-            )
-            for which, (source, target) in enumerate(
-                ((hidden_ref, got_hidden), (cotan_ref, got_cotan))
-            )
+    def block_copy(stream, k, which, device):
+        source, target = ((hidden_ref, got_hidden), (cotan_ref, got_cotan))[which]
+        return send(
+            source.at[:, k],
+            target.at[stream, :, k],
+            block_send.at[stream, k, which],
+            got_sem.at[stream, k, which],
+            device,
         )
 
     @pl.loop(0, CHUNKS)
     def _(k):
-        for copy in block_copies(FAR, k, far_id):
-            copy.start()
-        for copy in block_copies(NEAR, k, partner_id):
-            copy.start()
-
-    def wait_block(stream, k):
-        for copy in block_copies(stream, k, partner_id):
-            copy.wait_recv()
-
-    def unit_of(n):
+        for which in (LEFT, RIGHT):
+            block_copy(FAR, k, which, far_id).start()
+        for which in (LEFT, RIGHT):
+            block_copy(NEAR, k, which, partner_id).start()
+
+    def wait_block(stream, k, which):
+        block_copy(stream, k, which, partner_id).wait_recv()
+
+    ways = ((up, up_id, down, down_id), (down, down_id, up, up_id))
+
+    def first_copies(u, which, kind):
+        device = ways[which][1 + 2 * kind]
         return (
-            jnp.where(even, n // CHUNKS, lax.rem(n, 2)),
-            jnp.where(even, lax.rem(n, CHUNKS), n // 2),
-        )
-
-    def relayed_after(n):
-        late = jnp.where(n < CHUNKS + 2, n, n + 1)
-        paired = jnp.where(lax.rem(n, 2) == 0, n, n + 1)
-        return jnp.where(even, late, paired)
-
-    def first_copies(n, way):
-        device = (up_id, down_id)[way]
+            send(first_head.at[u, which, kind], first_head_in.at[u, which, kind], first_send.at[u, which, kind, 0], first_recv.at[u, which, kind, 0], device),
+            send(first_rest.at[u, which, kind], first_rest_in.at[u, which, kind], first_send.at[u, which, kind, 1], first_recv.at[u, which, kind, 1], device),
+        )
+
+    def pass_copies(u, which, straight=False):
+        device = across_id if straight else ways[which][1]
         return (
-            send(first_head.at[n, way], first_head_in.at[n, way], first_send.at[n, way, 0], first_recv.at[n, way, 0], device),
-            send(first_rest.at[n, way], first_rest_in.at[n, way], first_send.at[n, way, 1], first_recv.at[n, way, 1], device),
-        )
-
-    def pass_copies(n, way):
-        device = (up_id, down_id)[way]
-        return (
-            send(pass_head.at[n, way], pass_head_in.at[n, way], pass_send.at[n, way, 0], pass_recv.at[n, way, 0], device),
-            send(pass_rest.at[n, way], pass_rest_in.at[n, way], pass_send.at[n, way, 1], pass_recv.at[n, way, 1], device),
-        )
-
-    def rows_first(n, which, own, chunk):
+            send(pass_head.at[u, which], pass_head_in.at[u, which], pass_send.at[u, which, 0], pass_recv.at[u, which, 0], device),
+            send(pass_rest.at[u, which], pass_rest_in.at[u, which], pass_send.at[u, which, 1], pass_recv.at[u, which, 1], device),
+        )
+
+    own = (own_hidden, own_cotan)
+    got = (got_hidden, got_cotan)
+
+    def chunk_of(stream, k, which):
+        return got[which][stream, :, k].reshape(PARTS * piece, got[which].shape[-1])
+
+    def lanes_first(u, which, rows, chunk):
+        for part in range(PARTS):
+            gram[u, which, part] = contract(
+                rows[part * quarter : (part + 1) * quarter, :], chunk
+            )
+
+    def rows_first(u, which, columns, chunk):
         wide = 2 * LANES
         for block in range(block_rows // wide):
-            value = contract(chunk, own[block * wide : (block + 1) * wide, :])
+            value = contract(chunk, columns[block * wide : (block + 1) * wide, :])
             for part in range(PARTS):
                 for half in range(2):
                     start = (2 * block + half) * piece
-                    gram[n, which, part, start : start + piece, :] = value[
+                    gram[u, which, part, start : start + piece, :] = value[
                         part * piece : (part + 1) * piece,
                         half * LANES : (half + 1) * LANES,
                     ]
 
-    def compute(n, tile, k):
-        def chunk_of(got, stream):
-            return got[stream, :, k].reshape(PARTS * piece, got.shape[-1])
-
-        pairs = ((own_hidden, got_hidden), (own_cotan, got_cotan))
-
-        @pl.when(even)
-        def _():
-            for which, (own, got) in enumerate(pairs):
-                chunk = chunk_of(got, tile)
-                for part in range(PARTS):
-                    gram[n, which, part] = contract(
-                        own[part * quarter : (part + 1) * quarter, :], chunk
-                    )
-
-        @pl.when(jnp.logical_and(odd, tile == 0))
-        def _():
-            for which, (_, got) in enumerate(pairs):
-                other = got.at[NEAR].reshape(block_rows, got.shape[-1])
-                rows_first(n, which, other, chunk_of(got, FAR))
-
-        @pl.when(jnp.logical_and(odd, tile == 1))
-        def _():
-            for which, (own, got) in enumerate(pairs):
-                rows_first(n, which, own, chunk_of(got, FAR))
-
-        pack(gram[n, LEFT, across], first_head.at[n, UP, 0], first_rest.at[n, UP, 0])
-        pack(gram[n, RIGHT, up], first_head.at[n, UP, 1], first_rest.at[n, UP, 1])
-        pack(gram[n, RIGHT, across], first_head.at[n, DOWN, 0], first_rest.at[n, DOWN, 0])
-        pack(gram[n, LEFT, down], first_head.at[n, DOWN, 1], first_rest.at[n, DOWN, 1])
-        for way in (UP, DOWN):
-            for copy in first_copies(n, way):
+    def hand_on(u, which, straight=False):
+        if straight:
+            pack(gram[u, which, across], pass_head.at[u, which], pass_rest.at[u, which])
+            for copy in pass_copies(u, which, straight):
                 copy.start()
-
-    def relay(n):
-        for way, which, onward in ((UP, LEFT, up), (DOWN, RIGHT, down)):
-            for copy in first_copies(n, way):
+        relayed = ways[which][0] if straight else across
+        for kind, part in ((RELAY, relayed), (DIRECT, ways[which][2])):
+            pack(
+                gram[u, which, part],
+                first_head.at[u, which, kind],
+                first_rest.at[u, which, kind],
+            )
+            for copy in first_copies(u, which, kind):
+                copy.start()
+
+    def relay(u, which):
+        for copy in first_copies(u, which, RELAY):
+            copy.wait_recv()
+        total = gram[u, which, ways[which][0]] + unpack(
+            first_head_in.at[u, which, RELAY], first_rest_in.at[u, which, RELAY]
+        )
+        pack(total, pass_head.at[u, which], pass_rest.at[u, which])
+        for copy in pass_copies(u, which):
+            copy.start()
+
+    def whole(u, which, straight=False):
+        for copy in first_copies(u, which, DIRECT):
+            copy.wait_recv()
+        direct = unpack(
+            first_head_in.at[u, which, DIRECT], first_rest_in.at[u, which, DIRECT]
+        )
+        mine = gram[u, which, me] + direct
+        if straight:
+            for copy in first_copies(u, which, RELAY):
                 copy.wait_recv()
-            total = gram[n, which, onward] + unpack(
-                first_head_in.at[n, way, 0], first_rest_in.at[n, way, 0]
+            mine = mine + unpack(
+                first_head_in.at[u, which, RELAY], first_rest_in.at[u, which, RELAY]
             )
-            pack(total, pass_head.at[n, way], pass_rest.at[n, way])
-            for copy in pass_copies(n, way):
-                copy.start()
-
-    def finish(n):
-        tile, k = unit_of(n)
-        for way in (UP, DOWN):
-            for copy in pass_copies(n, way):
-                copy.wait_recv()
-        left, right = (
-            gram[n, which, me]
-            + unpack(pass_head_in.at[n, way], pass_rest_in.at[n, way])
-            + unpack(first_head_in.at[n, 1 - way, 1], first_rest_in.at[n, 1 - way, 1])
-            for which, way in ((LEFT, UP), (RIGHT, DOWN))
-        )
-        row_sums[tile * CHUNKS + k, : quarter // TOKENS, :] = jnp.sum(
-            (left * right).reshape(quarter // TOKENS, TOKENS, LANES), axis=1
-        )
+        for copy in pass_copies(u, which):
+            copy.wait_recv()
+        return mine + unpack(pass_head_in.at[u, which], pass_rest_in.at[u, which])
+
+    def finish(u, straight=False):
+        product = whole(u, LEFT, straight) * whole(u, RIGHT, straight)
+        row_sums[u, : quarter // TOKENS, :] = jnp.sum(
+            product.reshape(quarter // TOKENS, TOKENS, LANES), axis=1
+        )
+
+    def sent(u):
+        for which in (LEFT, RIGHT):
+            for kind in (RELAY, DIRECT):
+                for copy in first_copies(u, which, kind):
+                    copy.wait_send()
+            for copy in pass_copies(u, which):
+                copy.wait_send()
+
+    def block_sent(k):
+        for stream in (NEAR, FAR):
+            for which in (LEFT, RIGHT):
+                block_copy(stream, k, which, partner_id).wait_send()
 
     def epilogue(tile):
         sums = row_sums[pl.ds(tile * CHUNKS, CHUNKS)].reshape(CHUNKS * TOKENS, LANES)
@@ -276,74 +276,124 @@
     for load in loads:
         load.wait()
 
+    @pl.when(even)
+    def _():
+        @pl.loop(0, CHUNKS)
+        def _(k):
+            for which in (LEFT, RIGHT):
+                wait_block(NEAR, k, which)
+                lanes_first(k, which, own[which], chunk_of(NEAR, k, which))
+                hand_on(k, which)
+
+            @pl.when(k >= 1)
+            def _():
+                relay(k - 1, LEFT)
+                relay(k - 1, RIGHT)
+
+            @pl.when(k >= 2)
+            def _():
+                finish(k - 2)
+
+        relay(CHUNKS - 1, LEFT)
+        relay(CHUNKS - 1, RIGHT)
+
+        @pl.loop(0, CHUNKS - 1)
+        def _(k):
+            u = CHUNKS + k
+            for which in (LEFT, RIGHT):
+                wait_block(FAR, k, which)
+                lanes_first(u, which, own[which], chunk_of(FAR, k, which))
+                hand_on(u, which)
+
+            @pl.when(k == 1)
+            def _():
+                finish(CHUNKS - 2)
+                finish(CHUNKS - 1)
+                epilogue(0)
+                swapped.start()
+
+            for which in (LEFT, RIGHT):
+                relay(u, which)
+
+            @pl.when(k >= 1)
+            def _():
+                finish(u - 1)
+                sent(k - 1)
+                sent(u - 1)
+                block_sent(k - 1)
+
+        for which in (LEFT, RIGHT):
+            wait_block(FAR, CHUNKS - 1, which)
+            chunk = chunk_of(FAR, CHUNKS - 1, which)
+            lanes_first(units - 1, which, own[which], chunk)
+            hand_on(units - 1, which, straight=True)
+        finish(units - 2)
+        sent(CHUNKS - 2)
+        sent(units - 2)
+        block_sent(CHUNKS - 2)
+        sent(CHUNKS - 1)
+        finish(units - 1, straight=True)
+        epilogue(1)
+        moved.start()
+
     @pl.when(odd)
     def _():
         @pl.loop(0, CHUNKS)
         def _(k):
-            wait_block(NEAR, k)
-
-    @pl.loop(0, units)
-    def _(n):
-        tile, k = unit_of(n)
-
-        @pl.when(jnp.logical_or(even, tile == 0))
-        def _():
-            wait_block(jnp.where(even, tile, FAR), k)
-
-        compute(n, tile, k)
-
-        @pl.loop(jnp.where(n > 0, relayed_after(n - 1), 0), relayed_after(n))
-        def _(m):
-            relay(m)
-
-        @pl.when(n >= 2)
-        def _():
-            finish(n - 2)
-
-        @pl.when(jnp.logical_and(even, n == CHUNKS + 2))
-        def _():
-            epilogue(0)
-            swapped.start()
-
-    finish(units - 2)
+            for which in (LEFT, RIGHT):
+                wait_block(NEAR, k, which)
+
+        @pl.loop(0, CHUNKS)
+        def _(k):
+            for which in (LEFT, RIGHT):
+                wait_block(FAR, k, which)
+                chunk = chunk_of(FAR, k, which)
+                other = got[which].at[NEAR].reshape(block_rows, got[which].shape[-1])
+                rows_first(k, which, other, chunk)
+                hand_on(k, which)
+                rows_first(CHUNKS + k, which, own[which], chunk)
+                hand_on(CHUNKS + k, which)
+
+            for which in (LEFT, RIGHT):
+                relay(k, which)
+                relay(CHUNKS + k, which)
+
+            @pl.when(k >= 1)
+            def _():
+                finish(k - 1)
+                finish(CHUNKS + k - 1)
+                sent(k - 1)
+                sent(CHUNKS + k - 1)
+                block_sent(k - 1)
+
+        finish(CHUNKS - 1)
+        epilogue(0)
+        swapped.start()
+        finish(units - 1)
+        epilogue(1)
+
+    block_sent(CHUNKS - 1)
+    sent(units - 1)
 
     @pl.when(odd)
     def _():
-        epilogue(0)
-        swapped.start()
-
-    finish(units - 1)
-    epilogue(1)
-
-    @pl.when(even)
+        sent(CHUNKS - 1)
+
+    def put(offset, value):
+        for i in range(quarter // TOKENS):
+            out_ref[i, offset : offset + 1, :] = value[i : i + 1, :]
+
+    @pl.when(odd)
     def _():
-        moved.start()
-
-    @pl.loop(0, CHUNKS)
-    def _(k):
-        for stream in (NEAR, FAR):
-            for copy in block_copies(stream, k, partner_id):
-                copy.wait_send()
-
-    @pl.loop(0, units)
-    def _(n):
-        for way in (UP, DOWN):
-            for copy in first_copies(n, way):
-                copy.wait_send()
-            for copy in pass_copies(n, way):
-                copy.wait_send()
+        put(1, result[1])
 
     swapped.wait()
-    out_ref[0] = landed[0]
+    put(0, landed[0])
 
     @pl.when(even)
     def _():
         moved.wait()
-        out_ref[1] = landed[1]
-
-    @pl.when(odd)
-    def _():
-        out_ref[1] = result[1]
+        put(1, landed[1])
 
 
 def build_picks(even, lane_pick, keep, row_pick):
@@ -400,7 +450,7 @@
         held = pltpu.MemorySpace.HBM
         sums = pl.pallas_call(
             functools.partial(tile_kernel, grid_rows, grid_cols),
-            out_shape=jax.ShapeDtypeStruct((2, 16, LANES), f32),
+            out_shape=jax.ShapeDtypeStruct((samples // PARTS, 2, LANES), f32),
             in_specs=[pl.BlockSpec(memory_space=held)] * 2,
             out_specs=pl.BlockSpec(memory_space=pltpu.VMEM),
             scratch_shapes=[
@@ -426,8 +476,8 @@
                 dma((2,)),
                 dma((2, CHUNKS, 2)),
                 dma((2, CHUNKS, 2)),
-                dma((units, 2, 2)),
-                dma((units, 2, 2)),
+                dma((units, 2, 2, 2)),
+                dma((units, 2, 2, 2)),
                 dma((units, 2, 2)),
                 dma((units, 2, 2)),
                 dma((2,)),
@@ -443,8 +493,9 @@
             cotangent.reshape(PARTS, CHUNKS, piece, cotan_width),
         )
         kernel_scale = 1.0 / (tokens * math.sqrt(FF * D))
-        live = tile_live[0].astype(f32)[:, None, None] * kernel_scale
-        return (sums[:, : samples // PARTS, :samples] * live)[None]
+        values = sums[:, :, :samples] * kernel_scale
+        live = lax.broadcast_in_dim(tile_live[0], values.shape, (1,))
+        return jnp.transpose(values * live.astype(f32), (1, 0, 2))[None]
 
     return jax.shard_map(
         per_device,

time: 97.4 us -> 93.4 us (0.959)
  Pallas kernels: 95.1 us -> 91.2 us
    pallas_call x1, Pallas kernels: 95.1 us -> 91.2 us  [per_device(): pl.pallas_call(functools.partial(tile_kernel, grid_rows, grid_cols), out_...]
where the time goes in v3:
time: 93.4 us; the launch traced here: 93.3 us
  Pallas kernels  91.2 us (98%)
  other arithmetic  2.04 us (2%)
    pallas_call x1, Pallas kernels, per_device(): pl.pallas_call(functools.partial(tile_kernel, grid_rows, grid_cols), out_...  91.2 us

profile of v3, /device:TPU:2, one launch (start us, length us, event | category | flops | bytes accessed | tf_op | source)
XLA Modules:
  0.0 93.3 jit_solution(12988918568124001532)
XLA Ops:
  0.0 0.7 multiply_bitcast_fusion.1
  0.7 91.2 %shard_map.37 = f32[12,2,128]{2,1,0:T(2,128)} custom-call(bf16[4,6,32,2752]{3,2,1,0:T(8,128)(2,1)} %bitcast.8, bf16[4,6,32,1024]{3,2,1,0:T(8,128)(2,1)} %bitcast.9), custom_call_target="tpu_custom_call" | custom-call | tf_op jit(solution)/shard_map/pallas_call | solution.py:451
  91.9 1.4 %multiply_bitcast_fusion = f32[1,2,12,48]{3,1,2,0:T(2,128)} fusion(f32[12,2,128]{2,1,0:T(2,128)} %shard_map.37, f32[2]{0:T(128)S(1)} %multiply_bitcast_fusion.1), kind=kLoop, calls=%fused_computation | loop fusion | flops 1152 | bytes 9224 | tf_op jit(solution)/shard_map/broadcast_in_dim | solution.py:498

commit v4 on v3

--- a/solution.py
+++ b/solution.py
@@ -53,6 +53,8 @@
 def tile_kernel(
     grid_rows,
     grid_cols,
+    kernel_scale,
+    live_ref,
     hidden_ref,
     cotan_ref,
     out_ref,
@@ -60,6 +62,8 @@
     own_cotan,
     got_hidden,
     got_cotan,
+    edge,
+    edge_in,
     gram,
     first_head,
     first_rest,
@@ -76,6 +80,8 @@
     result,
     landed,
     load_sem,
+    edge_send,
+    edge_recv,
     block_send,
     got_sem,
     first_send,
@@ -95,6 +101,10 @@
     block_rows = own_hidden.shape[0]
     quarter = block_rows // PARTS
     piece = quarter // CHUNKS
+    half_rows = block_rows // 2
+    even_width = hidden_ref.shape[-1] // LANES * LANES
+    spare = hidden_ref.shape[-1] - even_width
+    assert 2 * spare == LANES
 
     up = lax.rem(me + 1, PARTS)
     down = lax.rem(me + PARTS - 1, PARTS)
@@ -145,20 +155,47 @@
 
     def block_copy(stream, k, which, device):
         source, target = ((hidden_ref, got_hidden), (cotan_ref, got_cotan))[which]
+        source, target = source.at[:, k], target.at[stream, :, k]
+        if stream == FAR and which == LEFT:
+            source, target = source.at[:, :, :even_width], target.at[:, :, :even_width]
         return send(
-            source.at[:, k],
-            target.at[stream, :, k],
+            source,
+            target,
             block_send.at[stream, k, which],
             got_sem.at[stream, k, which],
             device,
         )
 
+    edge_copy = send(edge, edge_in, edge_send, edge_recv, far_id)
+
+    for which in (LEFT, RIGHT):
+        block_copy(FAR, 0, which, far_id).start()
+
     @pl.loop(0, CHUNKS)
     def _(k):
         for which in (LEFT, RIGHT):
+            block_copy(NEAR, k, which, partner_id).start()
+
+    for load in loads:
+        load.wait()
+    edge[...] = jnp.concatenate(
+        [own_hidden[:half_rows, even_width:], own_hidden[half_rows:, even_width:]],
+        axis=1,
+    )
+    edge_copy.start()
+
+    @pl.loop(1, CHUNKS)
+    def _(k):
+        for which in (LEFT, RIGHT):
             block_copy(FAR, k, which, far_id).start()
-        for which in (LEFT, RIGHT):
-            block_copy(NEAR, k, which, partner_id).start()
+
+    def place_edge():
+        edge_copy.wait()
+        for half in range(2):
+            columns = edge_in[:, half * spare : (half + 1) * spare]
+            got_hidden[FAR, 2 * half : 2 * half + 2, :, :, even_width:] = columns.reshape(
+                2, CHUNKS, piece, spare
+            )
 
     def wait_block(stream, k, which):
         block_copy(stream, k, which, partner_id).wait_recv()
@@ -273,8 +310,6 @@
 
     row_sums[...] = jnp.zeros_like(row_sums)
     build_picks(even, lane_pick, keep, row_pick)
-    for load in loads:
-        load.wait()
 
     @pl.when(even)
     def _():
@@ -296,6 +331,8 @@
 
         relay(CHUNKS - 1, LEFT)
         relay(CHUNKS - 1, RIGHT)
+
+        place_edge()
 
         @pl.loop(0, CHUNKS - 1)
         def _(k):
@@ -343,6 +380,8 @@
             for which in (LEFT, RIGHT):
                 wait_block(NEAR, k, which)
 
+        place_edge()
+
         @pl.loop(0, CHUNKS)
         def _(k):
             for which in (LEFT, RIGHT):
@@ -380,6 +419,7 @@
         sent(CHUNKS - 1)
 
     def put(offset, value):
+        value = value * (live_ref[0, offset].astype(jnp.float32) * kernel_scale)
         for i in range(quarter // TOKENS):
             out_ref[i, offset : offset + 1, :] = value[i : i + 1, :]
 
@@ -448,16 +488,20 @@
         f32, bf16, i16 = jnp.float32, jnp.bfloat16, jnp.int16
         vmem, dma = pltpu.VMEM, pltpu.SemaphoreType.DMA
         held = pltpu.MemorySpace.HBM
+        kernel_scale = 1.0 / (tokens * math.sqrt(FF * D))
         sums = pl.pallas_call(
-            functools.partial(tile_kernel, grid_rows, grid_cols),
+            functools.partial(tile_kernel, grid_rows, grid_cols, kernel_scale),
             out_shape=jax.ShapeDtypeStruct((samples // PARTS, 2, LANES), f32),
-            in_specs=[pl.BlockSpec(memory_space=held)] * 2,
+            in_specs=[pl.BlockSpec(memory_space=pltpu.SMEM)]
+            + [pl.BlockSpec(memory_space=held)] * 2,
             out_specs=pl.BlockSpec(memory_space=pltpu.VMEM),
             scratch_shapes=[
                 vmem((block_rows, width), bf16),
                 vmem((block_rows, cotan_width), bf16),
                 vmem((2, PARTS, CHUNKS, piece, width), bf16),
                 vmem((2, PARTS, CHUNKS, piece, cotan_width), bf16),
+                vmem((block_rows // 2, LANES), bf16),
+                vmem((block_rows // 2, LANES), bf16),
                 vmem((units, 2, PARTS, quarter, LANES), f32),
                 vmem((units, 2, 2, quarter, LANES), bf16),
                 vmem((units, 2, 2, quarter // 2, LANES), i16),
@@ -474,6 +518,8 @@
                 vmem((2, TOKENS, LANES), f32),
                 vmem((2, TOKENS, LANES), f32),
                 dma((2,)),
+                dma,
+                dma,
                 dma((2, CHUNKS, 2)),
                 dma((2, CHUNKS, 2)),
                 dma((units, 2, 2, 2)),
@@ -489,13 +535,11 @@
                 vmem_limit_bytes=60 * 1024 * 1024,
             ),
         )(
+            tile_live,
             hidden.reshape(PARTS, CHUNKS, piece, width),
             cotangent.reshape(PARTS, CHUNKS, piece, cotan_width),
         )
-        kernel_scale = 1.0 / (tokens * math.sqrt(FF * D))
-        values = sums[:, :, :samples] * kernel_scale
-        live = lax.broadcast_in_dim(tile_live[0], values.shape, (1,))
-        return jnp.transpose(values * live.astype(f32), (1, 0, 2))[None]
+        return jnp.transpose(sums[:, :, :samples], (1, 0, 2))[None]
 
     return jax.shard_map(
         per_device,

time: 93.4 us -> 92.7 us (level)
  other arithmetic: 2.04 us -> 0 us
  local copies, waits for them, and re-layouts: 0 us -> 1.31 us
    broadcast_in_dim x1 -> x0, other arithmetic: 1.38 us -> none  [per_device(): return jnp.transpose(values * live.astype(f32), (1, 0, 2))[None]]
    broadcast_in_dim x0 -> x1, local copies, waits for them, and re-layouts: none -> 1.31 us  [per_device(): return jnp.transpose(sums[:, :, :samples], (1, 0, 2))[None]]
where the time goes in v4:
time: 92.7 us; the launch traced here: 91.8 us
  Pallas kernels  90.5 us (98%)
  local copies, waits for them, and re-layouts  1.31 us (1%)
    pallas_call x1, Pallas kernels, per_device(): pl.pallas_call(functools.partial(tile_kernel, grid_rows, grid_cols, kerne...  90.5 us

profile of v4, /device:TPU:2, one launch (start us, length us, event | category | flops | bytes accessed | tf_op | source)
XLA Modules:
  0.0 91.8 jit_solution(1532341282559741317)
XLA Ops:
  0.0 90.5 %shard_map.37 = f32[12,2,128]{2,1,0:T(2,128)} custom-call(s32[1,2]{1,0:T(1,128)} %live_ref.1, bf16[4,6,32,2752]{3,2,1,0:T(8,128)(2,1)} %bitcast.6, bf16[4,6,32,1024]{3,2,1,0:T(8,128)(2,1)} %bitcast.7), custom_call_target="tpu_custom_call" | custom-call | tf_op jit(solution)/shard_map/pallas_call | solution.py:492
  90.5 1.3 %slice_bitcast_fusion = f32[1,2,12,48]{3,1,2,0:T(2,128)} fusion(f32[12,2,128]{2,1,0:T(2,128)} %shard_map.37), kind=kLoop, calls=%fused_computation | loop fusion | bytes 9216 | tf_op jit(solution)/shard_map/broadcast_in_dim | solution.py:542

commit v5 on v4

--- a/solution.py
+++ b/solution.py
@@ -168,12 +168,12 @@
 
     edge_copy = send(edge, edge_in, edge_send, edge_recv, far_id)
 
-    for which in (LEFT, RIGHT):
+    for which in (RIGHT, LEFT):
         block_copy(FAR, 0, which, far_id).start()
 
     @pl.loop(0, CHUNKS)
     def _(k):
-        for which in (LEFT, RIGHT):
+        for which in (RIGHT, LEFT):
             block_copy(NEAR, k, which, partner_id).start()
 
     for load in loads:
@@ -186,7 +186,7 @@
 
     @pl.loop(1, CHUNKS)
     def _(k):
-        for which in (LEFT, RIGHT):
+        for which in (RIGHT, LEFT):
             block_copy(FAR, k, which, far_id).start()
 
     def place_edge():
@@ -289,7 +289,7 @@
         )
 
     def sent(u):
-        for which in (LEFT, RIGHT):
+        for which in (RIGHT, LEFT):
             for kind in (RELAY, DIRECT):
                 for copy in first_copies(u, which, kind):
                     copy.wait_send()
@@ -298,7 +298,7 @@
 
     def block_sent(k):
         for stream in (NEAR, FAR):
-            for which in (LEFT, RIGHT):
+            for which in (RIGHT, LEFT):
                 block_copy(stream, k, which, partner_id).wait_send()
 
     def epilogue(tile):
@@ -315,7 +315,7 @@
     def _():
         @pl.loop(0, CHUNKS)
         def _(k):
-            for which in (LEFT, RIGHT):
+            for which in (RIGHT, LEFT):
                 wait_block(NEAR, k, which)
                 lanes_first(k, which, own[which], chunk_of(NEAR, k, which))
                 hand_on(k, which)
@@ -337,7 +337,7 @@
         @pl.loop(0, CHUNKS - 1)
         def _(k):
             u = CHUNKS + k
-            for which in (LEFT, RIGHT):
+            for which in (RIGHT, LEFT):
                 wait_block(FAR, k, which)
                 lanes_first(u, which, own[which], chunk_of(FAR, k, which))
                 hand_on(u, which)
@@ -349,7 +349,7 @@
                 epilogue(0)
                 swapped.start()
 
-            for which in (LEFT, RIGHT):
+            for which in (RIGHT, LEFT):
                 relay(u, which)
 
             @pl.when(k >= 1)
@@ -359,7 +359,7 @@
                 sent(u - 1)
                 block_sent(k - 1)
 
-        for which in (LEFT, RIGHT):
+        for which in (RIGHT, LEFT):
             wait_block(FAR, CHUNKS - 1, which)
             chunk = chunk_of(FAR, CHUNKS - 1, which)
             lanes_first(units - 1, which, own[which], chunk)
@@ -377,14 +377,14 @@
     def _():
         @pl.loop(0, CHUNKS)
         def _(k):
-            for which in (LEFT, RIGHT):
+            for which in (RIGHT, LEFT):
                 wait_block(NEAR, k, which)
 
         place_edge()
 
         @pl.loop(0, CHUNKS)
         def _(k):
-            for which in (LEFT, RIGHT):
+            for which in (RIGHT, LEFT):
                 wait_block(FAR, k, which)
                 chunk = chunk_of(FAR, k, which)
                 other = got[which].at[NEAR].reshape(block_rows, got[which].shape[-1])
@@ -393,7 +393,7 @@
                 rows_first(CHUNKS + k, which, own[which], chunk)
                 hand_on(CHUNKS + k, which)
 
-            for which in (LEFT, RIGHT):
+            for which in (RIGHT, LEFT):
                 relay(k, which)
                 relay(CHUNKS + k, which)
 

time: 92.7 us -> 91.8 us (level)
  no operation moved by 1% of the time
where the time goes in v5:
time: 91.8 us; the launch traced here: 91.7 us
  Pallas kernels  90.3 us (98%)
  local copies, waits for them, and re-layouts  1.31 us (1%)
    pallas_call x1, Pallas kernels, per_device(): pl.pallas_call(functools.partial(tile_kernel, grid_rows, grid_cols, kerne...  90.3 us

profile of v5, /device:TPU:2, one launch (start us, length us, event | category | flops | bytes accessed | tf_op | source)
XLA Modules:
  0.0 91.7 jit_solution(9312607807118429579)
XLA Ops:
  0.0 90.3 %shard_map.37 = f32[12,2,128]{2,1,0:T(2,128)} custom-call(s32[1,2]{1,0:T(1,128)} %live_ref.1, bf16[4,6,32,2752]{3,2,1,0:T(8,128)(2,1)} %bitcast.6, bf16[4,6,32,1024]{3,2,1,0:T(8,128)(2,1)} %bitcast.7), custom_call_target="tpu_custom_call" | custom-call | tf_op jit(solution)/shard_map/pallas_call | solution.py:492
  90.4 1.3 %slice_bitcast_fusion = f32[1,2,12,48]{3,1,2,0:T(2,128)} fusion(f32[12,2,128]{2,1,0:T(2,128)} %shard_map.37), kind=kLoop, calls=%fused_computation | loop fusion | bytes 9216 | tf_op jit(solution)/shard_map/broadcast_in_dim | solution.py:542
